TPU v7x, 1024 devices: a whole 8x8x8 slice. The times are simulated.
1024 devices in a mesh: segment: 8 (over z), frame: 32 (over x_hi, y), row: 4 (over x_lo, core).
Axes of the slice: x: 8 (x_hi: 4, x_lo: 2; x = x_hi * 2 + x_lo), y: 8, z: 8, core: 2. Of those that a mesh axis runs over, the one named last changes fastest.
Arguments:
- clip_tokens: bfloat16 [8, 32, 4, 2, 64, 1536], P('segment', 'frame', 'row'), may hold values from -6 to 6
- qkv_weight: bfloat16 [8, 1536, 2304], P('segment'), may hold values from -1 to 1
- out_weight: bfloat16 [8, 768, 1536], P('segment'), may hold values from -0.21875 to 0.21875
- modulation: bfloat16 [8, 8, 3, 1536], P('segment'), may hold values from -4 to 4
- domain_ids: int32 [8], P('segment'), may hold values from 0 to 7
- tile_lists: int32 [32, 4, 2, 6], P('frame', 'row'), may hold values from 0 to 9, as said below
Outputs:
- handed: bfloat16 [8, 32, 4, 2, 64, 1536], P('segment', 'frame', 'row')
Inputs may be any that keep to these rules, and one draw needn't show every extreme that they name: `tile_lists`: each row names 6 different candidates, always the tile's own one, and never a tile outside the grid.
All inputs are finite; a program needn't handle non-finite values.
Results may differ from a plain program's by a relative error of at most 0.0081.
Values may be sent and summed in bfloat16 or wider, within the bound.
A program may use at most 32 MiB of HBM per device.

v0:
```python
import jax
import jax.numpy as jnp
from jax import lax
from jax.sharding import PartitionSpec as P

HD = 128


epsilon = 1e-06


def extended_2(cells, sides, width):
    for axis, dim in sides:
        count = lax.axis_size(axis)
        ends = count - 1
        head = lax.slice_in_dim(cells, 0, width, axis=dim)
        tail = lax.slice_in_dim(cells, cells.shape[dim] - width, cells.shape[dim], axis=dim)
        cells = jnp.concatenate(
            [
                lax.ppermute(tail, axis, [(i, (i + 1) % count) for i in range(ends)]),
                cells,
                lax.ppermute(head, axis, [((i + 1) % count, i) for i in range(ends)]),
            ],
            axis=dim,
        )
    return cells


def passed_along(x, axis, by):
    size = lax.axis_size(axis)
    return lax.ppermute(x, axis, [(i, (i + by) % size) for i in range(size)])


def normalize(rows, modulate):
    values = rows.astype(jnp.float32)
    row_mean = jnp.mean(values, axis=-1, keepdims=True)
    centered = values - row_mean
    row_var = jnp.mean(centered * centered, axis=-1, keepdims=True)
    scaled = centered * lax.rsqrt(row_var + epsilon)
    return (scaled * (1.0 + modulate[1]) + modulate[0]).astype(jnp.bfloat16)


def nearby(extended):
    return jnp.stack(
        [extended[1, 1], extended[0, 1], extended[2, 1], extended[1, 0], extended[1, 2]]
    )


def body(clip_tokens, qkv_weight, out_weight, modulation, domain_ids, tile_lists):
    col_tiles = clip_tokens.shape[3]
    tile_len = clip_tokens.shape[4]
    model_width = clip_tokens.shape[5]
    inner_width = out_weight.shape[1]
    head_count = inner_width // HD
    own_count = col_tiles * tile_len
    own_rows = clip_tokens.reshape(own_count, model_width)
    domain_count = modulation.shape[1]
    one_hot = (jnp.arange(domain_count, dtype=jnp.int32) == domain_ids[0]).astype(jnp.float32)
    table_rows = modulation[0].reshape(domain_count, 3 * model_width).astype(jnp.float32)
    modulate = jnp.dot(one_hot[None, :], table_rows, precision=lax.Precision.HIGHEST).reshape(
        3, model_width
    )
    weight = qkv_weight[0]
    normed = normalize(own_rows, modulate)
    projected = jnp.dot(normed, weight, preferred_element_type=jnp.float32)
    queries = projected[:, :inner_width].astype(jnp.bfloat16)
    pairs = projected[:, inner_width:].astype(jnp.bfloat16)
    slab = pairs.reshape(1, 1, col_tiles, tile_len, 2 * inner_width)
    extended = extended_2(slab, (("frame", 0), ("row", 1)), 1)
    candidates = nearby(extended).reshape(5 * col_tiles, tile_len, 2 * inner_width)
    chosen = tile_lists[0, 0]
    picked = candidates[chosen].reshape(col_tiles, -1, 2 * inner_width)
    key_count = picked.shape[1]
    key_rows = picked[..., :inner_width].reshape(col_tiles, key_count, head_count, HD)
    value_rows = picked[..., inner_width:].reshape(col_tiles, key_count, head_count, HD)
    query_rows = queries.reshape(col_tiles, tile_len, head_count, HD)
    scores = jnp.einsum(
        "tqhd,tkhd->thqk", query_rows, key_rows, preferred_element_type=jnp.float32
    ) * HD ** (-0.5)
    row_peak = jnp.max(scores, axis=-1, keepdims=True)
    raised = jnp.exp(scores - row_peak)
    attn_weights = (raised / jnp.sum(raised, axis=-1, keepdims=True)).astype(jnp.bfloat16)
    mixed_heads = jnp.einsum(
        "thqk,tkhd->tqhd", attn_weights, value_rows, preferred_element_type=jnp.float32
    )
    mixed_heads = mixed_heads.astype(jnp.bfloat16).reshape(own_count, inner_width)
    branch = jnp.dot(mixed_heads, out_weight[0], preferred_element_type=jnp.float32)
    finished = (
        (own_rows.astype(jnp.float32) + modulate[2] * branch)
        .astype(jnp.bfloat16)
        .reshape(clip_tokens.shape)
    )
    return passed_along(finished, "segment", 1)


def solution(mesh):
    return jax.shard_map(
        body,
        mesh=mesh,
        in_specs=(
            P("segment", "frame", "row", None, None, None),
            P("segment", None, None),
            P("segment", None, None),
            P("segment", None, None, None),
            P("segment"),
            P("frame", "row", None, None),
        ),
        out_specs=P("segment", "frame", "row", None, None, None),
        check_vma=False,
    )
```

profile of v0, /device:TPU:117, one launch (start us, length us, event | category | flops | bytes accessed | tf_op | source)
XLA Modules:
  0.0 102.0 jit_solution(13036076288924031557)
XLA Ops:
  0.8 1.1 %convolution_reduce_fusion = f32[4608]{0:T(1024)S(1)} fusion(bf16[8,4608]{1,0:T(8,128)(2,1)} %bitcast.64, s32[]{:T(128)} %bitcast.52), kind=kOutput, calls=%fused_computation.16 | convolution fusion | flops 73736 | bytes 92164 | tf_op jit(solution)/shard_map/dot_general | solution.py:60
  1.9 1.1 %convert_reduce_fusion = f32[2,64]{1,0:T(2,128)S(1)} fusion(bf16[1,1,1,2,64,1536]{5,4,3,2,1,0:T(8,128)(2,1)} %param.6), kind=kLoop, calls=%fused_computation.19 | loop fusion | flops 393088 | bytes 393728 | tf_op jit(solution)/shard_map/reduce_sum | solution.py:36
  3.1 1.3 %multiply_reduce_fusion = f32[2,64]{1,0:T(2,128)S(1)} fusion(bf16[1,1,1,2,64,1536]{5,4,3,2,1,0:T(8,128)(2,1)} %param.6, f32[2,64]{1,0:T(2,128)S(1)} %broadcast_multiply_fusion), kind=kLoop, calls=%fused_computation.18 | loop fusion | flops 786304 | bytes 394240 | tf_op jit(solution)/shard_map/reduce_sum | solution.py:38
  4.6 4.1 %fusion.3 = bf16[128,2304]{1,0:T(8,128)(2,1)S(1)} fusion(bf16[128,1536]{1,0:T(8,128)(2,1)S(1)} %bitcast.60, bf16[1,1536,2304]{2,1,0:T(8,128)(2,1)} %param.7), kind=kOutput, calls=%fused_computation.4 | convolution fusion | flops 906264576 | bytes 8060928 | tf_op jit(solution)/shard_map/dot_general | solution.py:65
  8.8 3.7 %collective-permute-start = (bf16[1,1,2,64,1536]{4,3,2,1,0:T(8,128)(2,1)S(1)}, bf16[1,1,2,64,1536]{4,3,2,1,0:T(8,128)(2,1)S(1)}, u32[]{:S(2)}, u32[]{:S(2)}) collective-permute-start(bf16[1,1,2,64,1536]{4,3,2,1,0:T(8,128)(2,1)S(1)} %bitcast.56), channel_id=1, source_target_pairs={{0,4},{4,8},{8,12},{12,16},{16,20},{20,24},{24,28},{28,32},{32,36}... | collective-permute-start | bytes 1179656 | tf_op jit(solution)/shard_map/ppermute | solution.py:20
  12.5 1.9 %collective-permute-start.1 = (bf16[1,1,2,64,1536]{4,3,2,1,0:T(8,128)(2,1)S(1)}, bf16[1,1,2,64,1536]{4,3,2,1,0:T(8,128)(2,1)}, u32[]{:S(2)}, u32[]{:S(2)}) collective-permute-start(bf16[1,1,2,64,1536]{4,3,2,1,0:T(8,128)(2,1)S(1)} %bitcast.57), channel_id=1, source_target_pairs={{4,0},{8,4},{12,8},{16,12},{20,16},{24,20},{28,24},{32,28},{36,32}... | collective-permute-start | bytes 1179656 | tf_op jit(solution)/shard_map/ppermute | solution.py:22
  15.2 1.9 %reshape.127 = bf16[2,64,6,128]{3,2,1,0:T(8,128)(2,1)} reshape(bf16[128,768]{1,0:T(8,128)(2,1)} %slice.50) | data formatting | bytes 393216 | tf_op jit(solution)/shard_map/reshape | solution.py:76
  17.1 3.6 %collective-permute-done = bf16[1,1,2,64,1536]{4,3,2,1,0:T(8,128)(2,1)S(1)} collective-permute-done((bf16[1,1,2,64,1536]{4,3,2,1,0:T(8,128)(2,1)S(1)}, bf16[1,1,2,64,1536]{4,3,2,1,0:T(8,128)(2,1)S(1)}, u32[]{:S(2)}, u32[]{:S(2)}) %collective-permute-start) | collective-permute-done | bytes 393248 | tf_op jit(solution)/shard_map/ppermute | solution.py:20
  20.7 17.4 %collective-permute-done.1 = bf16[1,1,2,64,1536]{4,3,2,1,0:T(8,128)(2,1)} collective-permute-done((bf16[1,1,2,64,1536]{4,3,2,1,0:T(8,128)(2,1)S(1)}, bf16[1,1,2,64,1536]{4,3,2,1,0:T(8,128)(2,1)}, u32[]{:S(2)}, u32[]{:S(2)}) %collective-permute-start.1) | collective-permute-done | bytes 393248 | tf_op jit(solution)/shard_map/ppermute | solution.py:22
  38.1 1.1 %pad_maximum_fusion = bf16[3,1,2,64,1536]{4,3,2,1,0:T(8,128)(2,1)S(1)} fusion(bf16[1,1,2,64,1536]{4,3,2,1,0:T(8,128)(2,1)} %collective-permute-done.1, bf16[1,1,2,64,1536]{4,3,2,1,0:T(8,128)(2,1)S(1)} %bitcast.58, bf16[1,1,2,64,1536]{4,3,2,1,0:T(8,128)(2,1)S(1)} %collective-permute-done), kind=kLoop, calls=%fused_computation.12 | loop fusion | flops 1179648 | bytes 2359296 | tf_op jit(solution)/shard_map/concatenate | solution.py:18
  39.2 1.9 %collective-permute-start.2 = (bf16[3,1,2,64,1536]{4,3,2,1,0:T(8,128)(2,1)S(1)}, bf16[3,1,2,64,1536]{4,3,2,1,0:T(8,128)(2,1)S(1)}, u32[]{:S(2)}, u32[]{:S(2)}) collective-permute-start(bf16[3,1,2,64,1536]{4,3,2,1,0:T(8,128)(2,1)S(1)} %pad_maximum_fusion), channel_id=1, source_target_pairs={{0,1},{1,2},{2,3},{4,5},{5,6},{6,7},{8,9},{9,10},{10,11},{12,13},{... | collective-permute-start | bytes 3538952 | tf_op jit(solution)/shard_map/ppermute | solution.py:20
  41.9 2.5 %collective-permute-start.3 = (bf16[3,1,2,64,1536]{4,3,2,1,0:T(8,128)(2,1)S(1)}, bf16[3,1,2,64,1536]{4,3,2,1,0:T(8,128)(2,1)S(1)}, u32[]{:S(2)}, u32[]{:S(2)}) collective-permute-start(bf16[3,1,2,64,1536]{4,3,2,1,0:T(8,128)(2,1)S(1)} %pad_maximum_fusion), channel_id=1, source_target_pairs={{1,0},{2,1},{3,2},{5,4},{6,5},{7,6},{9,8},{10,9},{11,10},{13,12},{... | collective-permute-start | bytes 3538952 | tf_op jit(solution)/shard_map/ppermute | solution.py:22
  45.2 1.8 %bitcast_dynamic-update-slice_fusion = bf16[5,2,64,1536]{3,2,1,0:T(8,128)(2,1)} fusion(bf16[5,2,64,1536]{3,2,1,0:T(8,128)(2,1)} %bitcast_dynamic-update-slice_fusion.1, bf16[1,1,2,64,1536]{4,3,2,1,0:T(8,128)(2,1)} %collective-permute-done.1), kind=kLoop, calls=%fused_computation.24 | loop fusion | bytes 786432
  46.9 7.3 %collective-permute-done.2 = bf16[3,1,2,64,1536]{4,3,2,1,0:T(8,128)(2,1)S(1)} collective-permute-done((bf16[3,1,2,64,1536]{4,3,2,1,0:T(8,128)(2,1)S(1)}, bf16[3,1,2,64,1536]{4,3,2,1,0:T(8,128)(2,1)S(1)}, u32[]{:S(2)}, u32[]{:S(2)}) %collective-permute-start.2) | collective-permute-done | bytes 1179680 | tf_op jit(solution)/shard_map/ppermute | solution.py:20
  55.0 4.4 %collective-permute-done.3 = bf16[3,1,2,64,1536]{4,3,2,1,0:T(8,128)(2,1)S(1)} collective-permute-done((bf16[3,1,2,64,1536]{4,3,2,1,0:T(8,128)(2,1)S(1)}, bf16[3,1,2,64,1536]{4,3,2,1,0:T(8,128)(2,1)S(1)}, u32[]{:S(2)}, u32[]{:S(2)}) %collective-permute-start.3) | collective-permute-done | bytes 1179680 | tf_op jit(solution)/shard_map/ppermute | solution.py:22
  60.2 3.7 %gather_fusion = bf16[12,64,1536]{2,1,0:T(8,128)(2,1)} fusion(bf16[10,64,1536]{2,1,0:T(8,128)(2,1)} %bitcast.12, s32[1024]{0:T(1024)S(1)} %pad_clamp_fusion), kind=kCustom, calls=%fused_computation | custom fusion | bytes 4718640 | tf_op jit(solution)/shard_map/gather | solution.py:72
  63.9 3.2 %fusion.22 = (bf16[2,384,768]{2,1,0:T(8,128)(2,1)}, bf16[2,384,768]{2,1,0:T(8,128)(2,1)}) fusion(bf16[2,384,1536]{2,1,0:T(8,128)(2,1)} %bitcast.53), kind=kLoop, calls=%fused_computation.40 | loop fusion | bytes 4718592 | tf_op jit(solution)/shard_map/slice | solution.py:74
  67.1 2.4 %copy.12 = bf16[2,384,768]{1,2,0:T(8,128)(2,1)} copy(bf16[2,384,768]{2,1,0:T(8,128)(2,1)} %get-tuple-element.6) | data formatting | bytes 2359296 | tf_op jit(solution)/shard_map/slice | solution.py:75
  69.5 2.4 %copy.13 = bf16[2,384,768]{1,2,0:T(8,128)(2,1)} copy(bf16[2,384,768]{2,1,0:T(8,128)(2,1)} %get-tuple-element.5) | data formatting | bytes 2359296 | tf_op jit(solution)/shard_map/slice | solution.py:74
  71.9 1.6 %convolution_multiply_fusion.1 = f32[2,6,64,384]{3,2,1,0:T(8,128)S(1)} fusion(bf16[2,384,6,128]{1,3,2,0:T(8,128)(2,1)} %bitcast.55, bf16[2,64,6,128]{3,2,1,0:T(8,128)(2,1)S(1)} %copy-done.3), kind=kOutput, calls=%fused_computation.10 | convolution fusion | flops 75792384 | bytes 2555904 | tf_op jit(solution)/shard_map/tqhd,tkhd->thqk/dot_general | solution.py:77
  73.5 1.0 %copy-done.2 = f32[2,6,64,384]{3,2,1,0:T(8,128)} copy-done((f32[2,6,64,384]{3,2,1,0:T(8,128)}, f32[2,6,64,384]{3,2,1,0:T(8,128)S(1)}, u32[]{:S(2)}) %copy-start.2) | copy-done | bytes 1179672
  74.9 3.4 %fusion.11 = bf16[2,64,6,128]{3,1,2,0:T(8,128)(2,1)S(1)} fusion(bf16[2,384,6,128]{1,3,2,0:T(8,128)(2,1)} %bitcast.61, f32[2,6,64]{2,1,0:T(8,128)S(1)} %fusion.23, f32[2,6,64,384]{3,2,1,0:T(8,128)} %copy-done.2), kind=kOutput, calls=%fused_computation.15 | convolution fusion | flops 76481664 | bytes 2558976 | tf_op jit(solution)/shard_map/thqk,tkhd->tqhd/dot_general | solution.py:83
  79.0 4.9 %collective-permute-start.4 = (bf16[1,1,1,2,64,1536]{5,4,3,2,1,0:T(8,128)(2,1)S(1)}, bf16[1,1,1,2,64,1536]{5,4,3,2,1,0:T(8,128)(2,1)S(1)}, u32[]{:S(2)}, u32[]{:S(2)}) collective-permute-start(bf16[1,1,1,2,64,1536]{5,4,3,2,1,0:T(8,128)(2,1)S(1)} %bitcast.63), channel_id=1, source_target_pairs={{0,128},{128,256},{256,384},{384,512},{512,640},{640,768},{768,896... | collective-permute-start | bytes 1179656 | tf_op jit(solution)/shard_map/ppermute | solution.py:31
  83.9 17.3 %collective-permute-done.4 = bf16[1,1,1,2,64,1536]{5,4,3,2,1,0:T(8,128)(2,1)S(1)} collective-permute-done((bf16[1,1,1,2,64,1536]{5,4,3,2,1,0:T(8,128)(2,1)S(1)}, bf16[1,1,1,2,64,1536]{5,4,3,2,1,0:T(8,128)(2,1)S(1)}, u32[]{:S(2)}, u32[]{:S(2)}) %collective-permute-start.4) | collective-permute-done | bytes 393248 | tf_op jit(solution)/shard_map/ppermute | solution.py:31
  (26 shorter events, 6.0 us)
Async XLA Ops:
  0.0 78.5 %copy-start = (bf16[1,768,1536]{2,1,0:T(8,128)(2,1)S(1)}, bf16[1,768,1536]{2,1,0:T(8,128)(2,1)}, u32[]{:S(2)}) copy-start(bf16[1,768,1536]{2,1,0:T(8,128)(2,1)} %param.8) | copy-start | bytes 7077892
  0.0 4.3 %copy-start.1 = (bf16[1,1,1,2,64,1536]{5,4,3,2,1,0:T(8,128)(2,1)S(1)}, bf16[1,1,1,2,64,1536]{5,4,3,2,1,0:T(8,128)(2,1)}, u32[]{:S(2)}) copy-start(bf16[1,1,1,2,64,1536]{5,4,3,2,1,0:T(8,128)(2,1)} %param.6) | copy-start | bytes 1179652
  8.8 6.3 %copy-start.4 = (s32[1,1,2,6]{3,2,1,0:T(2,128)S(1)}, s32[1,1,2,6]{3,2,1,0:T(2,128)}, u32[]{:S(2)}) copy-start(s32[1,1,2,6]{3,2,1,0:T(2,128)} %param.11) | copy-start | bytes 148
  8.8 11.9 %collective-permute-start = (bf16[1,1,2,64,1536]{4,3,2,1,0:T(8,128)(2,1)S(1)}, bf16[1,1,2,64,1536]{4,3,2,1,0:T(8,128)(2,1)S(1)}, u32[]{:S(2)}, u32[]{:S(2)}) collective-permute-start(bf16[1,1,2,64,1536]{4,3,2,1,0:T(8,128)(2,1)S(1)} %bitcast.56), channel_id=1, source_target_pairs={{0,4},{4,8},{8,12},{12,16},{16,20},{20,24},{24,28},{28,32},{32,36}... | collective-permute-start | bytes 1179656 | tf_op jit(solution)/shard_map/ppermute | solution.py:20
  12.5 25.6 %collective-permute-start.1 = (bf16[1,1,2,64,1536]{4,3,2,1,0:T(8,128)(2,1)S(1)}, bf16[1,1,2,64,1536]{4,3,2,1,0:T(8,128)(2,1)}, u32[]{:S(2)}, u32[]{:S(2)}) collective-permute-start(bf16[1,1,2,64,1536]{4,3,2,1,0:T(8,128)(2,1)S(1)} %bitcast.57), channel_id=1, source_target_pairs={{4,0},{8,4},{12,8},{16,12},{20,16},{24,20},{28,24},{32,28},{36,32}... | collective-permute-start | bytes 1179656 | tf_op jit(solution)/shard_map/ppermute | solution.py:22
  39.2 15.1 %collective-permute-start.2 = (bf16[3,1,2,64,1536]{4,3,2,1,0:T(8,128)(2,1)S(1)}, bf16[3,1,2,64,1536]{4,3,2,1,0:T(8,128)(2,1)S(1)}, u32[]{:S(2)}, u32[]{:S(2)}) collective-permute-start(bf16[3,1,2,64,1536]{4,3,2,1,0:T(8,128)(2,1)S(1)} %pad_maximum_fusion), channel_id=1, source_target_pairs={{0,1},{1,2},{2,3},{4,5},{5,6},{6,7},{8,9},{9,10},{10,11},{12,13},{... | collective-permute-start | bytes 3538952 | tf_op jit(solution)/shard_map/ppermute | solution.py:20
  41.9 17.5 %collective-permute-start.3 = (bf16[3,1,2,64,1536]{4,3,2,1,0:T(8,128)(2,1)S(1)}, bf16[3,1,2,64,1536]{4,3,2,1,0:T(8,128)(2,1)S(1)}, u32[]{:S(2)}, u32[]{:S(2)}) collective-permute-start(bf16[3,1,2,64,1536]{4,3,2,1,0:T(8,128)(2,1)S(1)} %pad_maximum_fusion), channel_id=1, source_target_pairs={{1,0},{2,1},{3,2},{5,4},{6,5},{7,6},{9,8},{10,9},{11,10},{13,12},{... | collective-permute-start | bytes 3538952 | tf_op jit(solution)/shard_map/ppermute | solution.py:22
  69.5 2.4 %copy-start.3 = (bf16[2,64,6,128]{3,2,1,0:T(8,128)(2,1)S(1)}, bf16[2,64,6,128]{3,2,1,0:T(8,128)(2,1)}, u32[]{:S(2)}) copy-start(bf16[2,64,6,128]{3,2,1,0:T(8,128)(2,1)} %reshape.127) | copy-start | bytes 589828
  73.5 1.1 %copy-start.2 = (f32[2,6,64,384]{3,2,1,0:T(8,128)}, f32[2,6,64,384]{3,2,1,0:T(8,128)S(1)}, u32[]{:S(2)}) copy-start(f32[2,6,64,384]{3,2,1,0:T(8,128)S(1)} %convolution_multiply_fusion.1) | copy-start | bytes 3538948
  79.0 22.2 %collective-permute-start.4 = (bf16[1,1,1,2,64,1536]{5,4,3,2,1,0:T(8,128)(2,1)S(1)}, bf16[1,1,1,2,64,1536]{5,4,3,2,1,0:T(8,128)(2,1)S(1)}, u32[]{:S(2)}, u32[]{:S(2)}) collective-permute-start(bf16[1,1,1,2,64,1536]{5,4,3,2,1,0:T(8,128)(2,1)S(1)} %bitcast.63), channel_id=1, source_target_pairs={{0,128},{128,256},{256,384},{384,512},{512,640},{640,768},{768,896... | collective-permute-start | bytes 1179656 | tf_op jit(solution)/shard_map/ppermute | solution.py:31
where the time goes:
time: 103 us; the launch traced here: 102 us
  waiting for transfers between devices  50 us (49%)
  local copies, waits for them, and re-layouts  21.2 us (21%)
  starting transfers between devices  14.9 us (14%)
  matrix products  10.7 us (10%)
  other arithmetic  4.2 us (4%)
    ppermute x2, waiting for transfers between devices, extended_2(): lax.ppermute(head, axis, [((i + 1) % count, i) for i in range(ends)])  21.8 us
    ppermute x1, waiting for transfers between devices, passed_along(): return lax.ppermute(x, axis, [(i, (i + by) % size) for i in range(size)])  17.3 us
    ppermute x2, waiting for transfers between devices, extended_2(): lax.ppermute(tail, axis, [(i, (i + 1) % count) for i in range(ends)])  11 us
    unnamed x15, local copies, waits for them, and re-layouts  5.89 us
    slice x2, local copies, waits for them, and re-layouts, body(): picked[..., :inner_width].reshape(col_tiles, key_count, head_count, HD)  5.6 us
    ppermute x2, starting transfers between devices, extended_2(): lax.ppermute(tail, axis, [(i, (i + 1) % count) for i in range(ends)])  5.58 us
    ppermute x1, starting transfers between devices, passed_along(): return lax.ppermute(x, axis, [(i, (i + by) % size) for i in range(size)])  4.91 us
    ppermute x2, starting transfers between devices, extended_2(): lax.ppermute(head, axis, [((i + 1) % count, i) for i in range(ends)])  4.39 us
  transfers between devices with their start and end apart: 5, of which 5 were waited for; matrix products, arithmetic and copies ran while one was open for 7% of the time, Pallas kernels for 0%

commit v1 on v0

v1 whole, which is shorter than its diff:
```python
import functools

import jax
import jax.numpy as jnp
from jax import lax
from jax.experimental import pallas as pl
from jax.experimental.pallas import tpu as pltpu
from jax.sharding import PartitionSpec as P

MESH = pl.DeviceIdType.MESH
HD = 128
HEADS = 6
INNER = HEADS * HD
D = 1536
ROWS = 128
TILE = 64
SLOTS = 5
KEYS = SLOTS * ROWS
NREL = 3
EPS = 1e-06
MASKED = -1e30


def kernel(
    n_frame, n_row, n_seg, group,
    dom_ref, x_hbm, w_hbm, wo_hbm, mod_hbm, lists_hbm,
    out_ref,
    x_v, normed, wkv, wq, wo, mod_v, lists_v,
    kv, relay, qs, bias, mixed, acc, fin,
    in_sem, wkv_sem, send_sem, recv_sem, rsend_sem, rrecv_sem, hand_send, hand_recv,
):
    f = lax.axis_index("frame")
    r = lax.axis_index("row")
    s = lax.axis_index("segment")
    y = lax.rem(f, group)
    g = lax.div(f, group)
    last_g = n_frame // group - 1

    small = [
        pltpu.make_async_copy(x_hbm, x_v, in_sem.at[0]),
        pltpu.make_async_copy(mod_hbm, mod_v, in_sem.at[1]),
        pltpu.make_async_copy(lists_hbm, lists_v, in_sem.at[3]),
    ]
    for c in small:
        c.start()
    kv_in = []
    for h in range(HEADS):
        pair = []
        for part in range(2):
            c = pltpu.make_async_copy(
                w_hbm.at[:, pl.ds(INNER * (1 + part) + HD * h, HD)],
                wkv.at[h, :, pl.ds(HD * part, HD)],
                wkv_sem.at[h, part],
            )
            c.start()
            pair.append(c)
        kv_in.append(pair)
    q_in = pltpu.make_async_copy(w_hbm.at[:, pl.ds(0, INNER)], wq, in_sem.at[4])
    q_in.start()
    wo_in = pltpu.make_async_copy(wo_hbm, wo, in_sem.at[5])
    wo_in.start()

    has_next = f < n_frame - 1
    has_prev = f > 0
    has_up = r < n_row - 1
    has_dn = r > 0
    edge_next = (y == group - 1) & (g < last_g)
    edge_prev = (y == 0) & (g > 0)
    relay_next = (y == 0) & (g < last_g)
    relay_prev = (y == group - 1) & (g > 0)

    barrier = pltpu.get_barrier_semaphore()
    peers = [
        (has_next, {"frame": f + 1}),
        (has_prev, {"frame": f - 1}),
        (has_up, {"row": r + 1}),
        (has_dn, {"row": r - 1}),
        (edge_next, {"frame": f - (group - 1)}),
        (edge_next, {"frame": f + group}),
        (edge_prev, {"frame": f + (group - 1)}),
        (edge_prev, {"frame": f - group}),
        (relay_next, {"frame": f + (group - 1)}),
        (relay_next, {"frame": f + group}),
        (relay_prev, {"frame": f - (group - 1)}),
        (relay_prev, {"frame": f - group}),
        (None, {"segment": lax.rem(s + n_seg - 1, n_seg)}),
    ]
    def when(cond):
        return (lambda act: act()) if cond is None else pl.when(cond)

    for cond, dev in peers:
        @when(cond)
        def _(dev=dev):
            pl.semaphore_signal(barrier, inc=1, device_id=dev, device_id_type=MESH)

    for cond, slot in ((f == 0, 1), (f == n_frame - 1, 2), (r == 0, 3), (r == n_row - 1, 4)):
        @pl.when(cond)
        def _(slot=slot):
            kv[slot] = jnp.zeros((HEADS, ROWS, 2 * HD), jnp.bfloat16)

    for c in small:
        c.wait()

    domains = mod_v.shape[1]
    mine = lax.broadcasted_iota(jnp.int32, (domains, D), 0) == dom_ref[0]

    def of_domain(i):
        return jnp.sum(jnp.where(mine, mod_v[i].astype(jnp.float32), 0.0), axis=0, keepdims=True)

    shift = of_domain(0)
    scale = 1.0 + of_domain(1)
    gate = of_domain(2)

    def norm_rows(i, _):
        rows = pl.ds(pl.multiple_of(i * 16, 16), 16)
        values = x_v[rows, :].astype(jnp.float32)
        mean = jnp.sum(values, axis=-1, keepdims=True) * (1.0 / D)
        centered = values - mean
        var = jnp.sum(centered * centered, axis=-1, keepdims=True) * (1.0 / D)
        normed[rows, :] = (centered * lax.rsqrt(var + EPS) * scale + shift).astype(jnp.bfloat16)
        return 0

    lax.fori_loop(0, ROWS // 16, norm_rows, 0, unroll=2)

    lists = lists_v[...]
    cand = lax.broadcasted_iota(jnp.int32, (2, KEYS), 1) // TILE
    hit = jnp.zeros((2, KEYS), jnp.float32)
    for j in range(lists.shape[1]):
        hit = jnp.where(cand == lists[:, j : j + 1], 1.0, hit)
    open_keys = jnp.where(hit > 0.5, 0.0, MASKED)
    for t in range(2):
        bias[pl.ds(t * TILE, TILE), :] = jnp.broadcast_to(open_keys[t : t + 1], (TILE, KEYS))

    greeted = 1
    for cond, _ in peers[:-1]:
        greeted += cond.astype(jnp.int32)
    pl.semaphore_wait(barrier, greeted)

    def copy_to(src, dst, send, recv, dev):
        return pltpu.make_async_remote_copy(
            src_ref=src, dst_ref=dst, send_sem=send, recv_sem=recv,
            device_id=dev, device_id_type=MESH,
        )

    def direct(slot, h, dev):
        return copy_to(kv.at[0, h], kv.at[slot, h], send_sem.at[slot - 1, h], recv_sem.at[slot - 1, h], dev)

    def to_relay(slot, h, dev):
        return copy_to(kv.at[0, h], relay.at[h], send_sem.at[slot - 1, h], rrecv_sem.at[h], dev)

    def onward(slot, h, dev):
        return copy_to(relay.at[h], kv.at[slot, h], rsend_sem.at[h], recv_sem.at[slot - 1, h], dev)

    for h in range(HEADS):
        for c in kv_in[h]:
            c.wait()
        kv[0, h] = jnp.dot(
            normed[...], wkv[h], preferred_element_type=jnp.float32
        ).astype(jnp.bfloat16)
        for has, edge, slot, near, via in (
            (has_next, edge_next, 1, f + 1, f - (group - 1)),
            (has_prev, edge_prev, 2, f - 1, f + (group - 1)),
        ):
            if h < NREL:
                @pl.when(edge)
                def _():
                    to_relay(slot, h, {"frame": via}).start()

                @pl.when(has & jnp.logical_not(edge))
                def _():
                    direct(slot, h, {"frame": near}).start()
            else:
                @pl.when(has)
                def _():
                    direct(slot, h, {"frame": near}).start()

        @pl.when(has_up)
        def _():
            direct(3, h, {"row": r + 1}).start()

        @pl.when(has_dn)
        def _():
            direct(4, h, {"row": r - 1}).start()

    q_in.wait()
    for p in range(HEADS // 2):
        both = jnp.dot(
            normed[...], wq[:, 2 * HD * p : 2 * HD * (p + 1)], preferred_element_type=jnp.float32
        ).astype(jnp.bfloat16)
        qs[2 * p] = both[:, :HD]
        qs[2 * p + 1] = both[:, HD:]

    for h in range(NREL):
        for cond, slot, dev in ((relay_next, 1, f + group), (relay_prev, 2, f - group)):
            @pl.when(cond)
            def _():
                to_relay(slot, h, {"frame": f}).wait_recv()
                onward(slot, h, {"frame": dev}).start()

    wo_in.wait()
    for h in range(HEADS):
        for cond, slot in ((has_prev, 1), (has_next, 2), (has_dn, 3), (has_up, 4)):
            @pl.when(cond)
            def _():
                direct(slot, h, {"frame": f}).wait_recv()
        keys = kv[:, h, :, :HD].reshape(KEYS, HD)
        values = kv[:, h, :, HD:].reshape(KEYS, HD)
        scores = lax.dot_general(
            qs[h], keys, (((1,), (1,)), ((), ())), preferred_element_type=jnp.float32
        ) * HD ** (-0.5) + bias[...]
        peak = jnp.max(scores, axis=-1, keepdims=True)
        raised = jnp.exp(scores - peak)
        total = jnp.sum(raised, axis=-1, keepdims=True)
        mix = jnp.dot(raised.astype(jnp.bfloat16), values, preferred_element_type=jnp.float32)
        mixed[:, HD * (h % 2) : HD * (h % 2 + 1)] = (mix / total).astype(jnp.bfloat16)
        if h % 2 == 1:
            part = jnp.dot(
                mixed[...], wo[HD * (h - 1) : HD * (h + 1), :], preferred_element_type=jnp.float32
            )
            if h == 1:
                acc[...] = part
            elif h < HEADS - 1:
                acc[...] += part
            else:
                fin[...] = (
                    x_v[...].astype(jnp.float32) + gate * (acc[...] + part)
                ).astype(jnp.bfloat16)

    hand = copy_to(fin, out_ref, hand_send, hand_recv, {"segment": lax.rem(s + 1, n_seg)})
    hand.start()

    for h in range(HEADS):
        for cond, slot in ((has_next, 1), (has_prev, 2), (has_up, 3), (has_dn, 4)):
            @pl.when(cond)
            def _():
                direct(slot, h, {"frame": f}).wait_send()
    for h in range(NREL):
        @pl.when(relay_next | relay_prev)
        def _():
            onward(1, h, {"frame": f}).wait_send()
    hand.wait()


def body(mesh, clip_tokens, qkv_weight, out_weight, modulation, domain_ids, tile_lists):
    any_space = pl.BlockSpec(memory_space=pl.ANY)
    bf16 = jnp.bfloat16
    dma = pltpu.SemaphoreType.DMA
    out = pl.pallas_call(
        functools.partial(
            kernel, mesh.shape["frame"], mesh.shape["row"], mesh.shape["segment"], 8
        ),
        out_shape=pltpu.VMEM((ROWS, D), bf16),
        in_specs=[pl.BlockSpec(memory_space=pltpu.SMEM)] + [any_space] * 5,
        out_specs=any_space,
        scratch_shapes=[
            pltpu.VMEM((ROWS, D), bf16),
            pltpu.VMEM((ROWS, D), bf16),
            pltpu.VMEM((HEADS, D, 2 * HD), bf16),
            pltpu.VMEM((D, INNER), bf16),
            pltpu.VMEM((INNER, D), bf16),
            pltpu.VMEM((3, modulation.shape[1], D), bf16),
            pltpu.VMEM(tile_lists.shape[2:], jnp.int32),
            pltpu.VMEM((SLOTS, HEADS, ROWS, 2 * HD), bf16),
            pltpu.VMEM((NREL, ROWS, 2 * HD), bf16),
            pltpu.VMEM((HEADS, ROWS, HD), bf16),
            pltpu.VMEM((ROWS, KEYS), jnp.float32),
            pltpu.VMEM((ROWS, 2 * HD), bf16),
            pltpu.VMEM((ROWS, D), jnp.float32),
            pltpu.VMEM((ROWS, D), bf16),
            dma((6,)),
            dma((HEADS, 2)),
            dma((4, HEADS)),
            dma((4, HEADS)),
            dma((NREL,)),
            dma((NREL,)),
            dma,
            dma,
        ],
        compiler_params=pltpu.CompilerParams(
            collective_id=0, has_side_effects=True, vmem_limit_bytes=24 * 2**20
        ),
        name="block",
    )(
        domain_ids,
        *(
            pltpu.with_memory_space_constraint(v, pltpu.HBM)
            for v in (
                clip_tokens.reshape(ROWS, D),
                qkv_weight[0],
                out_weight[0],
                jnp.transpose(modulation[0], (1, 0, 2)),
                tile_lists[0, 0],
            )
        ),
    )
    return out.reshape(clip_tokens.shape)


def solution(mesh):
    return jax.shard_map(
        functools.partial(body, mesh),
        mesh=mesh,
        in_specs=(
            P("segment", "frame", "row", None, None, None),
            P("segment", None, None),
            P("segment", None, None),
            P("segment", None, None, None),
            P("segment"),
            P("frame", "row", None, None),
        ),
        out_specs=P("segment", "frame", "row", None, None, None),
        check_vma=False,
    )
```

time: 103 us -> 50.2 us (0.49)
  the two profiles are of different devices: /device:TPU:117 before, /device:TPU:12 now
where the time goes in v1:
time: 50.2 us; the launch traced here: 50.1 us
  Pallas kernels  48.7 us (97%)
  local copies, waits for them, and re-layouts  0.75 us (1%)
  between operations  0.66 us (1%)
    pallas_call x1, Pallas kernels, body(): pl.pallas_call(functools.partial(kernel, mesh.shape['frame'], mesh.shape[...  48.7 us

profile of v1, /device:TPU:12, one launch (start us, length us, event | category | flops | bytes accessed | tf_op | source)
XLA Modules:
  0.0 50.1 jit_solution(13033658201839886377)
XLA Ops:
  0.7 48.7 %block.1 = bf16[128,1536]{1,0:T(8,128)(2,1)S(1)} custom-call(s32[1]{0:T(128)S(6)} %copy.9.dom_ref, bf16[128,1536]{1,0:T(8,128)(2,1)} %bitcast.11, bf16[1536,2304]{1,0:T(8,128)(2,1)} %bitcast.9, bf16[768,1536]{1,0:T(8,128)(2,1)} %bitcast.10, bf16[3,8,1536]{2,1,0:T(8,128)(2,1)} %bitcast.12, s32[2,6]{1,0:T(2,128)} %bitcast.13), custom_call_target="tpu_custom_call" | custom-call | tf_op jit(solution)/shard_map/block/pallas_call | solution.py:248
  49.4 0.7 %copy.8 = bf16[1,1,1,2,64,1536]{5,4,3,2,1,0:T(8,128)(2,1)} copy(bf16[1,1,1,2,64,1536]{5,4,3,2,1,0:T(8,128)(2,1)S(1)} %bitcast.8) | data formatting | bytes 786432

commit v2 on v1

--- a/solution.py
+++ b/solution.py
@@ -16,7 +16,8 @@
 TILE = 64
 SLOTS = 5
 KEYS = SLOTS * ROWS
-NREL = 3
+ROUTE = (1, 1, 2, 2, 0, 0)
+PARTS = 4
 EPS = 1e-06
 MASKED = -1e30
 
@@ -68,6 +69,8 @@
     edge_prev = (y == 0) & (g > 0)
     relay_next = (y == 0) & (g < last_g)
     relay_prev = (y == group - 1) & (g > 0)
+    back_next = (y == group - 2) & (g < last_g)
+    back_prev = (y == 1) & (g > 0)
 
     barrier = pltpu.get_barrier_semaphore()
     peers = [
@@ -83,6 +86,10 @@
         (relay_next, {"frame": f + group}),
         (relay_prev, {"frame": f - (group - 1)}),
         (relay_prev, {"frame": f - group}),
+        (edge_next, {"frame": f + 2}),
+        (edge_prev, {"frame": f - 2}),
+        (back_next, {"frame": f + 2}),
+        (back_prev, {"frame": f - 2}),
         (None, {"segment": lax.rem(s + n_seg - 1, n_seg)}),
     ]
     def when(cond):
@@ -150,6 +157,9 @@
 
     def onward(slot, h, dev):
         return copy_to(relay.at[h], kv.at[slot, h], rsend_sem.at[h], recv_sem.at[slot - 1, h], dev)
+
+    def back(slot, h, dev):
+        return copy_to(kv.at[3 - slot, h], kv.at[slot, h], rsend_sem.at[h], recv_sem.at[slot - 1, h], dev)
 
     for h in range(HEADS):
         for c in kv_in[h]:
@@ -161,18 +171,14 @@
             (has_next, edge_next, 1, f + 1, f - (group - 1)),
             (has_prev, edge_prev, 2, f - 1, f + (group - 1)),
         ):
-            if h < NREL:
+            if ROUTE[h] == 1:
                 @pl.when(edge)
                 def _():
                     to_relay(slot, h, {"frame": via}).start()
 
-                @pl.when(has & jnp.logical_not(edge))
-                def _():
-                    direct(slot, h, {"frame": near}).start()
-            else:
-                @pl.when(has)
-                def _():
-                    direct(slot, h, {"frame": near}).start()
+            @pl.when(has & jnp.logical_not(edge) if ROUTE[h] else has)
+            def _():
+                direct(slot, h, {"frame": near}).start()
 
         @pl.when(has_up)
         def _():
@@ -190,19 +196,35 @@
         qs[2 * p] = both[:, :HD]
         qs[2 * p + 1] = both[:, HD:]
 
-    for h in range(NREL):
-        for cond, slot, dev in ((relay_next, 1, f + group), (relay_prev, 2, f - group)):
-            @pl.when(cond)
-            def _():
-                to_relay(slot, h, {"frame": f}).wait_recv()
-                onward(slot, h, {"frame": dev}).start()
+    for h in range(HEADS):
+        if ROUTE[h] == 1:
+            for cond, slot, dev in ((relay_next, 1, f + group), (relay_prev, 2, f - group)):
+                @pl.when(cond)
+                def _():
+                    to_relay(slot, h, {"frame": f}).wait_recv()
+                    onward(slot, h, {"frame": dev}).start()
+        elif ROUTE[h] == 2:
+            for cond, slot, dev in ((back_next, 1, f + 2), (back_prev, 2, f - 2)):
+                @pl.when(cond)
+                def _():
+                    direct(3 - slot, h, {"frame": f}).wait_recv()
+                    back(slot, h, {"frame": dev}).start()
 
     wo_in.wait()
     for h in range(HEADS):
-        for cond, slot in ((has_prev, 1), (has_next, 2), (has_dn, 3), (has_up, 4)):
+        for cond, slot, taken in (
+            (has_prev, 1, back_prev),
+            (has_next, 2, back_next),
+            (has_dn, 3, None),
+            (has_up, 4, None),
+        ):
+            if ROUTE[h] == 2 and taken is not None:
+                cond = cond & jnp.logical_not(taken)
+
             @pl.when(cond)
             def _():
                 direct(slot, h, {"frame": f}).wait_recv()
+
         keys = kv[:, h, :, :HD].reshape(KEYS, HD)
         values = kv[:, h, :, HD:].reshape(KEYS, HD)
         scores = lax.dot_general(
@@ -213,32 +235,41 @@
         total = jnp.sum(raised, axis=-1, keepdims=True)
         mix = jnp.dot(raised.astype(jnp.bfloat16), values, preferred_element_type=jnp.float32)
         mixed[:, HD * (h % 2) : HD * (h % 2 + 1)] = (mix / total).astype(jnp.bfloat16)
-        if h % 2 == 1:
+        if h % 2 == 1 and h < HEADS - 1:
             part = jnp.dot(
                 mixed[...], wo[HD * (h - 1) : HD * (h + 1), :], preferred_element_type=jnp.float32
             )
-            if h == 1:
-                acc[...] = part
-            elif h < HEADS - 1:
-                acc[...] += part
-            else:
-                fin[...] = (
-                    x_v[...].astype(jnp.float32) + gate * (acc[...] + part)
-                ).astype(jnp.bfloat16)
-
-    hand = copy_to(fin, out_ref, hand_send, hand_recv, {"segment": lax.rem(s + 1, n_seg)})
-    hand.start()
-
-    for h in range(HEADS):
-        for cond, slot in ((has_next, 1), (has_prev, 2), (has_up, 3), (has_dn, 4)):
-            @pl.when(cond)
+            acc[...] = part if h == 1 else acc[...] + part
+
+    hands = []
+    for p in range(PARTS):
+        cols = pl.ds(D // PARTS * p, D // PARTS)
+        part = jnp.dot(mixed[...], wo[INNER - 2 * HD :, cols], preferred_element_type=jnp.float32)
+        fin[:, cols] = (
+            x_v[:, cols].astype(jnp.float32)
+            + gate[:, D // PARTS * p : D // PARTS * (p + 1)] * (acc[:, cols] + part)
+        ).astype(jnp.bfloat16)
+        c = copy_to(
+            fin.at[:, cols], out_ref.at[:, cols], hand_send.at[p], hand_recv.at[p],
+            {"segment": lax.rem(s + 1, n_seg)},
+        )
+        c.start()
+        hands.append(c)
+
+    for h in range(HEADS):
+        for has, edge, slot in ((has_next, edge_next, 1), (has_prev, edge_prev, 2), (has_up, None, 3), (has_dn, None, 4)):
+            if ROUTE[h] == 2 and edge is not None:
+                has = has & jnp.logical_not(edge)
+
+            @pl.when(has)
             def _():
                 direct(slot, h, {"frame": f}).wait_send()
-    for h in range(NREL):
-        @pl.when(relay_next | relay_prev)
-        def _():
-            onward(1, h, {"frame": f}).wait_send()
-    hand.wait()
+        if ROUTE[h]:
+            @pl.when((relay_next | relay_prev) if ROUTE[h] == 1 else (back_next | back_prev))
+            def _():
+                onward(1, h, {"frame": f}).wait_send()
+    for c in hands:
+        c.wait()
 
 
 def body(mesh, clip_tokens, qkv_weight, out_weight, modulation, domain_ids, tile_lists):
@@ -261,7 +292,7 @@
             pltpu.VMEM((3, modulation.shape[1], D), bf16),
             pltpu.VMEM(tile_lists.shape[2:], jnp.int32),
             pltpu.VMEM((SLOTS, HEADS, ROWS, 2 * HD), bf16),
-            pltpu.VMEM((NREL, ROWS, 2 * HD), bf16),
+            pltpu.VMEM((HEADS, ROWS, 2 * HD), bf16),
             pltpu.VMEM((HEADS, ROWS, HD), bf16),
             pltpu.VMEM((ROWS, KEYS), jnp.float32),
             pltpu.VMEM((ROWS, 2 * HD), bf16),
@@ -271,10 +302,10 @@
             dma((HEADS, 2)),
             dma((4, HEADS)),
             dma((4, HEADS)),
-            dma((NREL,)),
-            dma((NREL,)),
-            dma,
-            dma,
+            dma((HEADS,)),
+            dma((HEADS,)),
+            dma((PARTS,)),
+            dma((PARTS,)),
         ],
         compiler_params=pltpu.CompilerParams(
             collective_id=0, has_side_effects=True, vmem_limit_bytes=24 * 2**20

time: 50.2 us -> 48.9 us (0.974)
  the two profiles are of different devices: /device:TPU:12 before, /device:TPU:14 now
where the time goes in v2:
time: 48.9 us; the launch traced here: 48.8 us
  Pallas kernels  47.4 us (97%)
  local copies, waits for them, and re-layouts  0.75 us (2%)
  between operations  0.66 us (1%)
    pallas_call x1, Pallas kernels, body(): pl.pallas_call(functools.partial(kernel, mesh.shape['frame'], mesh.shape[...  47.4 us

profile of v2, /device:TPU:14, one launch (start us, length us, event | category | flops | bytes accessed | tf_op | source)
XLA Modules:
  0.0 48.8 jit_solution(14322785392874223198)
XLA Ops:
  0.7 47.4 %block.1 = bf16[128,1536]{1,0:T(8,128)(2,1)S(1)} custom-call(s32[1]{0:T(128)S(6)} %copy.9.dom_ref, bf16[128,1536]{1,0:T(8,128)(2,1)} %bitcast.11, bf16[1536,2304]{1,0:T(8,128)(2,1)} %bitcast.9, bf16[768,1536]{1,0:T(8,128)(2,1)} %bitcast.10, bf16[3,8,1536]{2,1,0:T(8,128)(2,1)} %bitcast.12, s32[2,6]{1,0:T(2,128)} %bitcast.13), custom_call_target="tpu_custom_call" | custom-call | tf_op jit(solution)/shard_map/block/pallas_call | solution.py:279
  48.0 0.7 %copy.8 = bf16[1,1,1,2,64,1536]{5,4,3,2,1,0:T(8,128)(2,1)} copy(bf16[1,1,1,2,64,1536]{5,4,3,2,1,0:T(8,128)(2,1)S(1)} %bitcast.8) | data formatting | bytes 786432

commit v3 on v2

--- a/solution.py
+++ b/solution.py
@@ -44,23 +44,6 @@
     ]
     for c in small:
         c.start()
-    kv_in = []
-    for h in range(HEADS):
-        pair = []
-        for part in range(2):
-            c = pltpu.make_async_copy(
-                w_hbm.at[:, pl.ds(INNER * (1 + part) + HD * h, HD)],
-                wkv.at[h, :, pl.ds(HD * part, HD)],
-                wkv_sem.at[h, part],
-            )
-            c.start()
-            pair.append(c)
-        kv_in.append(pair)
-    q_in = pltpu.make_async_copy(w_hbm.at[:, pl.ds(0, INNER)], wq, in_sem.at[4])
-    q_in.start()
-    wo_in = pltpu.make_async_copy(wo_hbm, wo, in_sem.at[5])
-    wo_in.start()
-
     has_next = f < n_frame - 1
     has_prev = f > 0
     has_up = r < n_row - 1
@@ -99,6 +82,23 @@
         @when(cond)
         def _(dev=dev):
             pl.semaphore_signal(barrier, inc=1, device_id=dev, device_id_type=MESH)
+
+    kv_in = []
+    for h in range(HEADS):
+        pair = []
+        for part in range(2):
+            c = pltpu.make_async_copy(
+                w_hbm.at[:, pl.ds(INNER * (1 + part) + HD * h, HD)],
+                wkv.at[h, :, pl.ds(HD * part, HD)],
+                wkv_sem.at[h, part],
+            )
+            c.start()
+            pair.append(c)
+        kv_in.append(pair)
+    q_in = pltpu.make_async_copy(w_hbm.at[:, pl.ds(0, INNER)], wq, in_sem.at[4])
+    q_in.start()
+    wo_in = pltpu.make_async_copy(wo_hbm, wo, in_sem.at[5])
+    wo_in.start()
 
     for cond, slot in ((f == 0, 1), (f == n_frame - 1, 2), (r == 0, 3), (r == n_row - 1, 4)):
         @pl.when(cond)

time: 48.9 us -> 48.4 us (0.990)
  the two profiles are of different devices: /device:TPU:14 before, /device:TPU:12 now
where the time goes in v3:
time: 48.4 us; the launch traced here: 48.3 us
  Pallas kernels  46.9 us (97%)
  local copies, waits for them, and re-layouts  0.75 us (2%)
  between operations  0.66 us (1%)
    pallas_call x1, Pallas kernels, body(): pl.pallas_call(functools.partial(kernel, mesh.shape['frame'], mesh.shape[...  46.9 us

profile of v3, /device:TPU:12, one launch (start us, length us, event | category | flops | bytes accessed | tf_op | source)
XLA Modules:
  0.0 48.3 jit_solution(3143682627444981828)
XLA Ops:
  0.7 46.9 %block.1 = bf16[128,1536]{1,0:T(8,128)(2,1)S(1)} custom-call(s32[1]{0:T(128)S(6)} %copy.9.dom_ref, bf16[128,1536]{1,0:T(8,128)(2,1)} %bitcast.11, bf16[1536,2304]{1,0:T(8,128)(2,1)} %bitcast.9, bf16[768,1536]{1,0:T(8,128)(2,1)} %bitcast.10, bf16[3,8,1536]{2,1,0:T(8,128)(2,1)} %bitcast.12, s32[2,6]{1,0:T(2,128)} %bitcast.13), custom_call_target="tpu_custom_call" | custom-call | tf_op jit(solution)/shard_map/block/pallas_call | solution.py:279
  47.5 0.7 %copy.8 = bf16[1,1,1,2,64,1536]{5,4,3,2,1,0:T(8,128)(2,1)} copy(bf16[1,1,1,2,64,1536]{5,4,3,2,1,0:T(8,128)(2,1)S(1)} %bitcast.8) | data formatting | bytes 786432
